TPU v7x, 256 devices: a whole 4x4x8 slice. The times are simulated.
256 devices in a mesh: dp: 8 (over y, core), expert: 32 (over x, z).
Axes of the slice: x: 4, y: 4, z: 8, core: 2. Of those that a mesh axis runs over, the one named last changes fastest.
Arguments:
- tokens: bfloat16 [2048, 4096], P(('dp', 'expert')), may hold values from -6 to 6
- expert_ids: int32 [2048, 8], P(('dp', 'expert')), may hold values from 0 to 31, all different within a row; in each aligned block of 8 rows (0 to 7, 8 to 15, ...) at most 3 rows name the same one
- gate_values: float32 [2048, 8], P(('dp', 'expert')), may hold values from 0.05 to 1
- w_gate: bfloat16 [32, 4096, 2048], P('expert', None, 'dp'), may hold values from -0.09375 to 0.09375
- w_up: bfloat16 [32, 4096, 2048], P('expert', None, 'dp'), may hold values from -0.09375 to 0.09375
- w_down: bfloat16 [32, 2048, 4096], P('expert', 'dp'), may hold values from -0.125 to 0.125
- s_gate: bfloat16 [4096, 2048], P(None, 'dp'), may hold values from -0.09375 to 0.09375
- s_up: bfloat16 [4096, 2048], P(None, 'dp'), may hold values from -0.09375 to 0.09375
- s_down: bfloat16 [2048, 4096], P('dp'), may hold values from -0.125 to 0.125
Outputs:
- mixed: bfloat16 [2048, 4096], P(('dp', 'expert'))
Inputs may be any that keep to these rules, and one draw needn't show every extreme that they name: `expert_ids`: each row names 8 different experts; the 8 rows of one device name one expert at most 3 times.
All inputs are finite; a program needn't handle non-finite values.
Results may differ from a plain program's by a relative error of at most 0.0054.
Values may be sent and summed in bfloat16 or wider, within the bound.
No kernel may reach another device: no remote copies, remote signals or barrier semaphores. Data moves between devices by JAX's collectives and lax.ppermute only.
A program may use at most 128 MiB of HBM per device.

v0:
```python
import jax
import jax.numpy as jnp
from jax import lax
from jax.sharding import PartitionSpec as P


def swiglu(rows, gate_w, up_w, down_w):
    gate = jnp.dot(rows, gate_w, preferred_element_type=jnp.float32)
    up = jnp.dot(rows, up_w, preferred_element_type=jnp.float32)
    hidden = (jax.nn.silu(gate) * up).astype(jnp.bfloat16)
    return jnp.dot(hidden, down_w, preferred_element_type=jnp.float32)


def slot_tables(route_ids, route_gates, experts, capacity):
    row_count, picks = route_ids.shape
    listed = route_ids.reshape(-1)
    expert_range = jnp.arange(experts, dtype=jnp.int32)
    marks = (listed[:, None] == expert_range[None, :]).astype(jnp.int32)
    earlier = jnp.cumsum(marks, axis=0) - marks
    position = jnp.sum(earlier * marks, axis=1)
    slot_index = (listed * capacity + position).reshape(row_count, picks)
    slot_range = jnp.arange(experts * capacity, dtype=jnp.int32)
    matches = slot_index[:, :, None] == slot_range[None, None, :]
    picker = jnp.any(matches, axis=1).astype(jnp.bfloat16)
    combiner = jnp.sum(jnp.where(matches, route_gates[:, :, None], jnp.float32(0.0)), axis=1)
    return (picker, combiner)


def dispatch_rows(picker, source_rows):
    placed = jnp.einsum("rs,rd->sd", picker, source_rows, preferred_element_type=jnp.float32)
    return placed.astype(jnp.bfloat16)


def per_device(tokens, expert_ids, gate_values, w_gate, w_up, w_down, s_gate, s_up, s_down):
    experts = lax.axis_size("expert")
    groups = lax.axis_size("dp")
    own_rows, width = tokens.shape
    picks = expert_ids.shape[1]
    capacity = max(2, min(own_rows, 3 * own_rows * picks // (2 * experts)))
    gate_local = w_gate[0]
    up_local = w_up[0]
    down_local = w_down[0]
    column = lax.all_gather(tokens, "dp", axis=0, tiled=True)
    column_ids, column_gates = (
        lax.all_gather(expert_ids, "dp", axis=0, tiled=True),
        lax.all_gather(gate_values, "dp", axis=0, tiled=True),
    )
    column_cap = capacity * groups
    picker, combiner = slot_tables(column_ids, column_gates, experts, column_cap)
    outgoing = dispatch_rows(picker, column).reshape(experts, column_cap, width)
    arrived = lax.all_to_all(outgoing, "expert", split_axis=0, concat_axis=0, tiled=True)
    items = arrived.shape[1]
    partial_value = swiglu(
        arrived.reshape(experts * items, width), gate_local, up_local, down_local
    )
    partial_value = partial_value.astype(jnp.bfloat16).reshape(experts, items, width)
    returned = lax.all_to_all(partial_value, "expert", split_axis=0, concat_axis=0, tiled=True)
    returned_rows = returned.reshape(experts * column_cap, width)
    routed = jnp.dot(
        combiner,
        returned_rows.astype(jnp.float32),
        precision=lax.Precision.HIGHEST,
        preferred_element_type=jnp.float32,
    )
    mixed = lax.psum_scatter(
        swiglu(column, s_gate, s_up, s_down) + routed, "dp", scatter_dimension=0, tiled=True
    )
    return mixed.astype(jnp.bfloat16)


def solution(mesh):
    placed = (
        P(("dp", "expert"), None),
        P(("dp", "expert"), None),
        P(("dp", "expert"), None),
        P("expert", None, "dp"),
        P("expert", None, "dp"),
        P("expert", "dp", None),
        P(None, "dp"),
        P(None, "dp"),
        P("dp", None),
    )
    return jax.shard_map(
        per_device, mesh=mesh, in_specs=placed, out_specs=P(("dp", "expert"), None), check_vma=False
    )
```

profile of v0, /device:TPU:2, one launch (start us, length us, event | category | flops | bytes accessed | tf_op | source)
XLA Modules:
  0.0 403.5 jit_solution(12211258155983552361)
XLA Ops:
  6.5 13.7 %all_gather.10 = s32[64,8]{1,0:T(8,128)S(1)} all-gather(s32[8,8]{1,0:T(8,128)} %param.10), channel_id=1, replica_groups=mesh['dp'=8,'expert'=32] {'dp'}, dimensions={0}, use_global_device_ids=true | all-gather | bytes 2304 | tf_op jit(solution)/shard_map/all_gather | solution.py:45
  20.2 0.1 eq.42
  20.3 0.1 eq.38
  20.4 1.2 reduce-window.6
  21.6 0.2 slice_reduce_fusion
  21.8 0.1 fusion.24
  22.0 0.1 reduce_sum.21
  22.1 0.5 fusion.5
  22.6 13.3 %all_gather.9 = bf16[64,4096]{1,0:T(8,128)(2,1)S(1)} all-gather(bf16[8,4096]{1,0:T(8,128)(2,1)} %param.9), channel_id=1, replica_groups=mesh['dp'=8,'expert'=32] {'dp'}, dimensions={0}, use_global_device_ids=true | all-gather | bytes 589824 | tf_op jit(solution)/shard_map/all_gather | solution.py:43
  35.9 1.8 convolution_convert_fusion
  37.8 150.5 %all_to_all.10 = bf16[32,24,4096]{2,1,0:T(8,128)(2,1)S(1)} all-to-all(bf16[32,24,4096]{2,1,0:T(8,128)(2,1)S(1)} %bitcast.49), channel_id=1, replica_groups=mesh['dp'=8,'expert'=32] {'expert'}, dimensions={0} | all-to-all | bytes 12582912 | tf_op jit(solution)/shard_map/all_to_all | solution.py:51
  188.3 2.7 copy-done.1
  191.0 2.7 fusion.3
  193.7 12.8 %convolution_convert_fusion.1 = bf16[768,4096]{1,0:T(8,128)(2,1)} fusion(bf16[1,256,4096]{2,1,0:T(8,128)(2,1)S(1)} %copy-done, bf16[768,4096]{1,0:T(8,128)(2,1)} %bitcast.52, bf16[1,4096,256]{2,1,0:T(8,128)(2,1)} %param.13, f32[768,256]{1,0:T(8,128)} %fusion.3), kind=kOutput, calls=%fused_computation.1 | convolution fusion | flops 3225550848 | bytes 17563648 | tf_op jit(solution)/shard_map/dot_general | solution.py:11
  206.5 7.8 %all-to-all-start.1 = ((bf16[32,24,4096]{2,1,0:T(8,128)(2,1)}), bf16[32,24,4096]{2,1,0:T(8,128)(2,1)}, u32[]{:S(2)}, u32[]{:S(2)}) async-start(bf16[32,24,4096]{2,1,0:T(8,128)(2,1)} %bitcast.50), calls=%async_computation.1 | async-start | bytes 12582912 | tf_op jit(solution)/shard_map/all_to_all | solution.py:57
  214.3 0.0 reduce-scatter.2.cloned.1.call-start
  214.4 13.1 %all_gather.11 = f32[64,8]{1,0:T(8,128)S(1)} all-gather(f32[8,8]{1,0:T(8,128)S(1)} %copy-done.2), channel_id=1, replica_groups=mesh['dp'=8,'expert'=32] {'dp'}, dimensions={0}, use_global_device_ids=true | all-gather | bytes 2304 | tf_op jit(solution)/shard_map/all_gather | solution.py:46
  227.5 0.5 select_reduce_fusion
  228.0 2.1 fusion.34
  230.1 4.7 %fusion.15 = f32[64,4096]{1,0:T(8,128)} fusion(bf16[256,4096]{1,0:T(8,128)(2,1)} %param.17, bf16[64,4096]{1,0:T(8,128)(2,1)S(1)} %all_gather.9, bf16[4096,256]{1,0:T(8,128)(2,1)} %param.16, f32[64,256]{1,0:T(8,128)S(1)} %fusion.34), kind=kOutput, calls=%fused_computation.15 | convolution fusion | flops 268533760 | bytes 5832704 | tf_op jit(solution)/shard_map/dot_general | solution.py:11
  234.7 115.3 %all-to-all-done.1 = bf16[32,24,4096]{2,1,0:T(8,128)(2,1)} async-done(((bf16[32,24,4096]{2,1,0:T(8,128)(2,1)}), bf16[32,24,4096]{2,1,0:T(8,128)(2,1)}, u32[]{:S(2)}, u32[]{:S(2)}) %all-to-all-start.1) | async-done | bytes 6291488 | tf_op jit(solution)/shard_map/all_to_all | solution.py:57
  350.0 7.5 %convolution_add_fusion = f32[64,4096]{1,0:T(8,128)} fusion(f32[64,4096]{1,0:T(8,128)} %fusion.15, f32[64,768]{1,0:T(8,128)S(1)} %select_reduce_fusion, bf16[768,4096]{1,0:T(8,128)(2,1)} %bitcast.7), kind=kOutput, calls=%fused_computation.2 | convolution fusion | flops 2416181248 | bytes 8585216 | tf_op jit(solution)/shard_map/dot_general | solution.py:59
  357.6 37.5 %reduce-scatter.2.cloned.1.call-done = f32[8,4096]{1,0:T(8,128)} async-done(((f32[64,4096]{1,0:T(8,128)}), f32[8,4096]{1,0:T(8,128)}) %reduce-scatter.2.cloned.1.call-update) | async-done | bytes 131088 | tf_op jit(solution)/shard_map/reduce_scatter | solution.py:65
  395.1 1.5 convert_element_type.30
  (12 shorter events, 0.1 us)
Async XLA Ops:
  6.5 187.2 %copy-start = (bf16[1,256,4096]{2,1,0:T(8,128)(2,1)S(1)}, bf16[1,256,4096]{2,1,0:T(8,128)(2,1)}, u32[]{:S(2)}) copy-start(bf16[1,256,4096]{2,1,0:T(8,128)(2,1)} %param.14) | copy-start | bytes 6291460
  37.8 153.2 %copy-start.3 = (bf16[1,4096,256]{2,1,0:T(8,128)(2,1)S(1)}, bf16[1,4096,256]{2,1,0:T(8,128)(2,1)}, u32[]{:S(2)}) copy-start(bf16[1,4096,256]{2,1,0:T(8,128)(2,1)} %param.12) | copy-start | bytes 6291460
  188.3 2.7 copy-start.1
  206.5 7.8 %copy-start.2 = (f32[8,8]{1,0:T(8,128)S(1)}, f32[8,8]{1,0:T(8,128)}, u32[]{:S(2)}) copy-start(f32[8,8]{1,0:T(8,128)} %param.11) | copy-start | bytes 772
  206.5 143.5 %all-to-all-start.1 = ((bf16[32,24,4096]{2,1,0:T(8,128)(2,1)}), bf16[32,24,4096]{2,1,0:T(8,128)(2,1)}, u32[]{:S(2)}, u32[]{:S(2)}) async-start(bf16[32,24,4096]{2,1,0:T(8,128)(2,1)} %bitcast.50), calls=%async_computation.1 | async-start | bytes 12582912 | tf_op jit(solution)/shard_map/all_to_all | solution.py:57
  214.3 180.8 %reduce-scatter.2.cloned.1.call-start = ((), (), s32[]{:S(2)}) async-start(), calls=%async_computation.3 | async-start | bytes 1179648 | tf_op jit(solution)/shard_map/reduce_scatter | solution.py:65
Sparse Core Ops, SparseCore 0:
  357.7 37.3 reduce-scatter.1
where the time goes:
time: 404 us; the launch traced here: 403 us
  blocking collectives  191 us (47%)
  waiting for transfers between devices  153 us (38%)
  matrix products  31.6 us (8%)
  between operations  13.5 us (3%)
  starting transfers between devices  7.82 us (2%)
    all_to_all x1, blocking collectives, per_device(): lax.all_to_all(outgoing, 'expert', split_axis=0, concat_axis=0, tiled=True)  151 us
    all_to_all x1, waiting for transfers between devices, per_device(): lax.all_to_all(partial_value, 'expert', split_axis=0, concat_axis=0, tile...  115 us
    reduce_scatter x1, waiting for transfers between devices, per_device(): lax.psum_scatter(swiglu(column, s_gate, s_up, s_down) + routed, 'dp', sca...  37.5 us
    dot_general x2, matrix products, swiglu(): return jnp.dot(hidden, down_w, preferred_element_type=jnp.float32)  17.5 us
    all_gather x1, blocking collectives, per_device(): lax.all_gather(expert_ids, 'dp', axis=0, tiled=True)  13.7 us
    all_gather x1, blocking collectives, per_device(): column = lax.all_gather(tokens, 'dp', axis=0, tiled=True)  13.3 us
    all_gather x1, blocking collectives, per_device(): lax.all_gather(gate_values, 'dp', axis=0, tiled=True)  13.1 us
  transfers between devices with their start and end apart: 2, of which 2 were waited for; matrix products, arithmetic and copies ran while one was open for 2% of the time, Pallas kernels for 0%

commit v1 on v0

v1 whole, which is shorter than its diff:
```python
import jax
import jax.numpy as jnp
from jax import lax
from jax.experimental import pallas as pl
from jax.experimental.pallas import tpu as pltpu
from jax.sharding import Mesh, PartitionSpec as P

CAP = 3
LANES = 128
SMEM = pltpu.SMEM
VMEM = pltpu.VMEM


def pack_rows(ids, rows3, experts):
    count, picks = ids.shape

    def kernel(ids_ref, rows_ref, out_ref, pos_ref, used_ref):
        out_ref[...] = jnp.zeros_like(out_ref)
        for e in range(experts):
            used_ref[e] = 0
        for r in range(count):
            row = rows_ref[r]
            for k in range(picks):
                e = ids_ref[r, k]
                n = used_ref[e]
                used_ref[e] = n + 1
                slot = e * CAP + n
                pos_ref[r, k] = slot
                out_ref[slot] = row

    return pl.pallas_call(
        kernel,
        out_shape=(
            jax.ShapeDtypeStruct((experts * CAP,) + rows3.shape[1:], rows3.dtype),
            jax.ShapeDtypeStruct(ids.shape, jnp.int32),
        ),
        in_specs=[pl.BlockSpec(memory_space=SMEM), pl.BlockSpec(memory_space=VMEM)],
        out_specs=(pl.BlockSpec(memory_space=VMEM), pl.BlockSpec(memory_space=SMEM)),
        scratch_shapes=[SMEM((experts,), jnp.int32)],
        name="pack_rows",
    )(ids, rows3)


def combine_rows(pos, gates, returned, shared3):
    count, picks = pos.shape

    def kernel(pos_ref, gates_ref, ret_ref, shared_ref, out_ref):
        for r in range(count):
            total = shared_ref[r]
            for k in range(picks):
                total = total + gates_ref[r, k] * ret_ref[pos_ref[r, k]].astype(jnp.float32)
            out_ref[r] = total.astype(out_ref.dtype)

    return pl.pallas_call(
        kernel,
        out_shape=jax.ShapeDtypeStruct(shared3.shape, jnp.bfloat16),
        in_specs=[
            pl.BlockSpec(memory_space=SMEM),
            pl.BlockSpec(memory_space=SMEM),
            pl.BlockSpec(memory_space=VMEM),
            pl.BlockSpec(memory_space=VMEM),
        ],
        out_specs=pl.BlockSpec(memory_space=VMEM),
        name="combine_rows",
    )(pos, gates, returned, shared3)


def hidden_of(rows, gate_w, up_w):
    gate = jnp.dot(rows, gate_w, preferred_element_type=jnp.float32)
    up = jnp.dot(rows, up_w, preferred_element_type=jnp.float32)
    return lax.optimization_barrier((jax.nn.silu(gate) * up).astype(jnp.bfloat16))


def shift(value, axis, by):
    n = lax.axis_size(axis)
    return lax.ppermute(value, axis, [(i, (i + by) % n) for i in range(n)])


def per_device(tokens, ids, gates, w_gate, w_up, w_down, s_gate, s_up, s_down):
    w_gate, w_up, w_down = w_gate[0], w_up[0], w_down[0]
    experts = lax.axis_size(("x", "z"))
    planes = lax.axis_size("y")
    own, width = tokens.shape
    folds = width // LANES
    slots = experts * CAP

    packed, pos = pack_rows(ids, tokens.reshape(own, folds, LANES), experts)
    arrived = lax.all_to_all(
        packed.reshape(experts, CAP, folds, LANES), ("x", "z"), split_axis=0, concat_axis=0, tiled=True
    )
    mine = jnp.concatenate([arrived.reshape(slots, width), tokens], axis=0)

    def ffn(rows):
        routed = jnp.dot(hidden_of(rows[:slots], w_gate, w_up), w_down, preferred_element_type=jnp.float32)
        shared = jnp.dot(hidden_of(rows[slots:], s_gate, s_up), s_down, preferred_element_type=jnp.float32)
        return jnp.concatenate([routed, shared], axis=0)

    blocks = [mine] + [shift(mine, "y", by) for by in range(1, planes)]
    total = None
    for by, block in enumerate(blocks):
        other = shift(block, "core", 1)
        back = shift(ffn(other).astype(jnp.bfloat16), "core", 1)
        both = ffn(block) + back.astype(jnp.float32)
        if by:
            both = shift(both.astype(jnp.bfloat16), "y", planes - by).astype(jnp.float32)
        total = both if total is None else total + both

    routed = total[:slots].astype(jnp.bfloat16).reshape(experts, CAP, folds, LANES)
    returned = lax.all_to_all(routed, ("x", "z"), split_axis=0, concat_axis=0, tiled=True)
    mixed = combine_rows(
        pos, gates, returned.reshape(slots, folds, LANES), total[slots:].reshape(own, folds, LANES)
    )
    return mixed.reshape(own, width)


def solution(mesh):
    fine = Mesh(mesh.devices.reshape(4, 2, 4, 8), ("y", "core", "x", "z"))
    dp, expert = ("y", "core"), ("x", "z")
    placed = (
        P(dp + expert, None),
        P(dp + expert, None),
        P(dp + expert, None),
        P(expert, None, dp),
        P(expert, None, dp),
        P(expert, dp, None),
        P(None, dp),
        P(None, dp),
        P(dp, None),
    )
    return jax.shard_map(
        per_device, mesh=fine, in_specs=placed, out_specs=P(dp + expert, None), check_vma=False
    )
```

time: 404 us -> 182 us (0.45)
  blocking collectives: 191 us -> 32.6 us
  waiting for transfers between devices: 153 us -> 87.4 us
  starting transfers between devices: 7.82 us -> 22.9 us
  between operations: 13.5 us -> 0.22 us
  matrix products: 31.6 us -> 20.6 us
  local copies, waits for them, and re-layouts: 3.17 us -> 9.26 us
    all_to_all x1, blocking collectives: 151 us -> 32.6 us  [per_device(): lax.all_to_all(packed.reshape(experts, CAP, folds, LANES), ('x', 'z'), sp...]
    all_to_all x1, waiting for transfers between devices: 115 us -> 19.4 us  [per_device(): lax.all_to_all(routed, ('x', 'z'), split_axis=0, concat_axis=0, tiled=True)]
    ppermute x0 -> x14, waiting for transfers between devices: none -> 68.1 us  [shift(): return lax.ppermute(value, axis, [(i, (i + by) % n) for i in range(n)])]
    all_gather x3 -> x0, blocking collectives: 40.1 us -> none  [the longest x1 13.7 us: per_device(): lax.all_gather(expert_ids, 'dp', axis=0, tiled=True)]
    reduce_scatter x1 -> x0, waiting for transfers between devices: 37.5 us -> none  [per_device(): lax.psum_scatter(swiglu(column, s_gate, s_up, s_down) + routed, 'dp', sca...]
    ppermute x0 -> x14, starting transfers between devices: none -> 13.4 us  [shift(): return lax.ppermute(value, axis, [(i, (i + by) % n) for i in range(n)])]
    dot_general x6 -> x48, matrix products: 31.6 us -> 20.6 us  [the longest x16 6.89 us: hidden_of(): up = jnp.dot(rows, up_w, preferred_element_type=jnp.float32)]
    unnamed x8 -> x23, local copies, waits for them, and re-layouts: 2.67 us -> 9.25 us
  transfers between devices with their start and end apart: 2 -> 15, of which waited for: 2 -> 6; matrix products, arithmetic and copies ran while one was open for 2% -> 11% of each run, Pallas kernels for 0% -> 0%
where the time goes in v1:
time: 182 us; the launch traced here: 180 us
  waiting for transfers between devices  87.4 us (48%)
  blocking collectives  32.6 us (18%)
  starting transfers between devices  22.9 us (13%)
  matrix products  20.6 us (11%)
  local copies, waits for them, and re-layouts  9.26 us (5%)
  Pallas kernels  3.98 us (2%)
  other arithmetic  2.64 us (1%)
    ppermute x14, waiting for transfers between devices, shift(): return lax.ppermute(value, axis, [(i, (i + by) % n) for i in range(n)])  68.1 us
    all_to_all x1, blocking collectives, per_device(): lax.all_to_all(packed.reshape(experts, CAP, folds, LANES), ('x', 'z'), sp...  32.6 us
    all_to_all x1, waiting for transfers between devices, per_device(): lax.all_to_all(routed, ('x', 'z'), split_axis=0, concat_axis=0, tiled=True)  19.4 us
    ppermute x14, starting transfers between devices, shift(): return lax.ppermute(value, axis, [(i, (i + by) % n) for i in range(n)])  13.4 us
    all_to_all x1, starting transfers between devices, per_device(): lax.all_to_all(routed, ('x', 'z'), split_axis=0, concat_axis=0, tiled=True)  9.41 us
    unnamed x23, local copies, waits for them, and re-layouts  9.25 us
    dot_general x16, matrix products, hidden_of(): up = jnp.dot(rows, up_w, preferred_element_type=jnp.float32)  6.89 us
    dot_general x16, matrix products, hidden_of(): gate = jnp.dot(rows, gate_w, preferred_element_type=jnp.float32)  6.84 us
  transfers between devices with their start and end apart: 15, of which 6 were waited for; matrix products, arithmetic and copies ran while one was open for 11% of the time, Pallas kernels for 0%

profile of v1, /device:TPU:2, one launch (start us, length us, event | category | flops | bytes accessed | tf_op | source)
XLA Modules:
  0.0 179.6 jit_solution(10776741505798834002)
XLA Ops:
  0.0 1.6 copy.29
  1.6 2.1 %pack_rows.1 = (bf16[96,32,128]{2,1,0:T(8,128)(2,1)}, s32[8,8]{1,0:T(8,128)}) custom-call(s32[8,8]{1,0:T(8,128)} %ids_ref.1, bf16[8,32,128]{2,1,0:T(8,128)(2,1)} %bitcast.145), custom_call_target="tpu_custom_call" | custom-call | tf_op jit(solution)/shard_map/pack_rows/pallas_call | solution.py:31
  3.8 32.6 %all_to_all.10 = bf16[32,3,32,128]{3,2,1,0:T(8,128)(2,1)S(1)} all-to-all(bf16[32,3,32,128]{3,2,1,0:T(8,128)(2,1)} %bitcast.143), channel_id=1, replica_groups=mesh['y'=4,'core'=2,'x'=4,'z'=8] {'x','z'}, dimensions={0} | all-to-all | bytes 1572864 | tf_op jit(solution)/shard_map/all_to_all | solution.py:88
  36.7 3.1 %collective-permute-start.10 = (bf16[104,4096]{1,0:T(8,128)(2,1)S(1)}, bf16[104,4096]{1,0:T(8,128)(2,1)S(1)}, u32[]{:S(2)}, u32[]{:S(2)}) collective-permute-start(bf16[104,4096]{1,0:T(8,128)(2,1)S(1)} %constant_dynamic-update-slice_fusion), channel_id=1, source_target_pairs={{0,192},{64,0},{128,64},{192,128},{1,193},{65,1},{129,65},{193,129... | collective-permute-start | bytes 2555912 | tf_op jit(solution)/shard_map/ppermute | solution.py:76
  40.9 1.3 collective-permute-start.6
  42.3 0.7 collective-permute-start.2
  42.9 30.6 %collective-permute-done.10 = bf16[104,4096]{1,0:T(8,128)(2,1)S(1)} collective-permute-done((bf16[104,4096]{1,0:T(8,128)(2,1)S(1)}, bf16[104,4096]{1,0:T(8,128)(2,1)S(1)}, u32[]{:S(2)}, u32[]{:S(2)}) %collective-permute-start.10) | collective-permute-done | bytes 852000 | tf_op jit(solution)/shard_map/ppermute | solution.py:76
  74.8 0.7 copy-done.7
  77.8 0.7 collective-permute-done.2
  86.6 0.7 collective-permute-done.11
  96.4 3.1 %collective-permute-start.5 = (bf16[104,4096]{1,0:T(8,128)(2,1)S(1)}, bf16[104,4096]{1,0:T(8,128)(2,1)S(1)}, u32[]{:S(2)}, u32[]{:S(2)}) collective-permute-start(bf16[104,4096]{1,0:T(8,128)(2,1)S(1)} %fusion.47), channel_id=1, source_target_pairs={{0,192},{64,0},{128,64},{192,128},{1,193},{65,1},{129,65},{193,129... | collective-permute-start | bytes 2555912 | tf_op jit(solution)/shard_map/ppermute | solution.py:76
  100.5 2.6 %collective-permute-start.13 = (bf16[104,4096]{1,0:T(8,128)(2,1)S(1)}, bf16[104,4096]{1,0:T(8,128)(2,1)S(1)}, u32[]{:S(2)}, u32[]{:S(2)}) collective-permute-start(bf16[104,4096]{1,0:T(8,128)(2,1)S(1)} %fusion.49), channel_id=1, source_target_pairs={{0,64},{64,128},{128,192},{192,0},{1,65},{65,129},{129,193},{193,1... | collective-permute-start | bytes 2555912 | tf_op jit(solution)/shard_map/ppermute | solution.py:76
  104.5 32.0 %collective-permute-done.5 = bf16[104,4096]{1,0:T(8,128)(2,1)S(1)} collective-permute-done((bf16[104,4096]{1,0:T(8,128)(2,1)S(1)}, bf16[104,4096]{1,0:T(8,128)(2,1)S(1)}, u32[]{:S(2)}, u32[]{:S(2)}) %collective-permute-start.5) | collective-permute-done | bytes 852000 | tf_op jit(solution)/shard_map/ppermute | solution.py:76
  136.5 4.0 %collective-permute-done.13 = bf16[104,4096]{1,0:T(8,128)(2,1)S(1)} collective-permute-done((bf16[104,4096]{1,0:T(8,128)(2,1)S(1)}, bf16[104,4096]{1,0:T(8,128)(2,1)S(1)}, u32[]{:S(2)}, u32[]{:S(2)}) %collective-permute-start.13) | collective-permute-done | bytes 852000 | tf_op jit(solution)/shard_map/ppermute | solution.py:76
  140.5 1.8 %fusion.46 = f32[104,4096]{1,0:T(8,128)} fusion(f32[8,4096]{1,0:T(8,128)S(1)} %fusion.105, f32[96,4096]{1,0:T(8,128)S(1)} %fusion.10, bf16[104,4096]{1,0:T(8,128)(2,1)S(1)} %collective-permute-done.13, bf16[104,4096]{1,0:T(8,128)(2,1)S(1)} %collective-permute-done.9, bf16[104,4096]{1,0:T(8,128)(2,1)S(1)} %collective-permute-done.5, ...), kind=kLoop, calls=%fused_computation.55 | loop fusion | flops 3833856 | bytes 6815744 | tf_op jit(solution)/shard_map/add | solution.py:106
  142.3 1.5 fusion.57
  143.9 1.1 copy.12
  145.0 9.4 %all-to-all-start.1 = ((bf16[32,3,32,128]{3,2,1,0:T(8,128)(2,1)}), bf16[32,3,32,128]{3,2,1,0:T(8,128)(2,1)S(1)}, u32[]{:S(2)}, u32[]{:S(2)}) async-start(bf16[32,3,32,128]{3,2,1,0:T(8,128)(2,1)} %bitcast.12), calls=%async_computation.1 | async-start | bytes 1572864 | tf_op jit(solution)/shard_map/all_to_all | solution.py:109
  154.4 0.9 slice_bitcast_fusion
  155.3 0.7 copy.27
  156.0 19.4 %all-to-all-done.1 = bf16[32,3,32,128]{3,2,1,0:T(8,128)(2,1)S(1)} async-done(((bf16[32,3,32,128]{3,2,1,0:T(8,128)(2,1)}), bf16[32,3,32,128]{3,2,1,0:T(8,128)(2,1)S(1)}, u32[]{:S(2)}, u32[]{:S(2)}) %all-to-all-start.1) | async-done | bytes 786464 | tf_op jit(solution)/shard_map/all_to_all | solution.py:109
  175.3 0.9 copy-done.5
  176.2 1.9 %combine_rows.1 = bf16[8,32,128]{2,1,0:T(8,128)(2,1)} custom-call(s32[8,8]{1,0:T(8,128)} %get-tuple-element.7.pos_ref, f32[8,8]{1,0:T(8,128)} %gates_ref.1, bf16[96,32,128]{2,1,0:T(8,128)(2,1)} %bitcast.141, f32[8,32,128]{2,1,0:T(8,128)} %bitcast.144), custom_call_target="tpu_custom_call" | custom-call | tf_op jit(solution)/shard_map/combine_rows/pallas_call | solution.py:54
  178.1 1.5 copy.28
  (89 shorter events, 24.5 us)
Async XLA Ops:
  0.0 83.1 %copy-start = (bf16[1,256,4096]{2,1,0:T(8,128)(2,1)S(1)}, bf16[1,256,4096]{2,1,0:T(8,128)(2,1)}, u32[]{:S(2)}) copy-start(bf16[1,256,4096]{2,1,0:T(8,128)(2,1)} %param.14) | copy-start | bytes 6291460
  0.0 36.6 %copy-start.6 = (bf16[8,4096]{1,0:T(8,128)(2,1)S(1)}, bf16[8,4096]{1,0:T(8,128)(2,1)}, u32[]{:S(2)}) copy-start(bf16[8,4096]{1,0:T(8,128)(2,1)} %param.9) | copy-start | bytes 196612
  3.7 36.0 %copy-start.1 = (bf16[4096,256]{1,0:T(8,128)(2,1)S(1)}, bf16[4096,256]{1,0:T(8,128)(2,1)}, u32[]{:S(2)}) copy-start(bf16[4096,256]{1,0:T(8,128)(2,1)} %param.15) | copy-start | bytes 6291460
  36.4 3.8 %copy-start.2 = (bf16[4096,256]{1,0:T(8,128)(2,1)S(1)}, bf16[4096,256]{1,0:T(8,128)(2,1)}, u32[]{:S(2)}) copy-start(bf16[4096,256]{1,0:T(8,128)(2,1)} %param.16) | copy-start | bytes 6291460
  36.7 3.9 %copy-start.3 = (bf16[256,4096]{1,0:T(8,128)(2,1)S(1)}, bf16[256,4096]{1,0:T(8,128)(2,1)}, u32[]{:S(2)}) copy-start(bf16[256,4096]{1,0:T(8,128)(2,1)} %param.17) | copy-start | bytes 6291460
  36.7 36.9 %collective-permute-start.10 = (bf16[104,4096]{1,0:T(8,128)(2,1)S(1)}, bf16[104,4096]{1,0:T(8,128)(2,1)S(1)}, u32[]{:S(2)}, u32[]{:S(2)}) collective-permute-start(bf16[104,4096]{1,0:T(8,128)(2,1)S(1)} %constant_dynamic-update-slice_fusion), channel_id=1, source_target_pairs={{0,192},{64,0},{128,64},{192,128},{1,193},{65,1},{129,65},{193,129... | collective-permute-start | bytes 2555912 | tf_op jit(solution)/shard_map/ppermute | solution.py:76
  40.9 33.4 %copy-start.4 = (bf16[1,4096,256]{2,1,0:T(8,128)(2,1)S(1)}, bf16[1,4096,256]{2,1,0:T(8,128)(2,1)}, u32[]{:S(2)}) copy-start(bf16[1,4096,256]{2,1,0:T(8,128)(2,1)} %param.12) | copy-start | bytes 6291460
  40.9 35.1 %collective-permute-start.6 = (bf16[104,4096]{1,0:T(8,128)(2,1)S(1)}, bf16[104,4096]{1,0:T(8,128)(2,1)S(1)}, u32[]{:S(2)}, u32[]{:S(2)}) collective-permute-start(bf16[104,4096]{1,0:T(8,128)(2,1)S(1)} %constant_dynamic-update-slice_fusion), channel_id=1, source_target_pairs={{0,128},{64,192},{128,0},{192,64},{1,129},{65,193},{129,1},{193,65... | collective-permute-start | bytes 2555912 | tf_op jit(solution)/shard_map/ppermute | solution.py:76
  42.3 36.2 %collective-permute-start.2 = (bf16[104,4096]{1,0:T(8,128)(2,1)S(1)}, bf16[104,4096]{1,0:T(8,128)(2,1)S(1)}, u32[]{:S(2)}, u32[]{:S(2)}) collective-permute-start(bf16[104,4096]{1,0:T(8,128)(2,1)S(1)} %constant_dynamic-update-slice_fusion), channel_id=1, source_target_pairs={{0,64},{64,128},{128,192},{192,0},{1,65},{65,129},{129,193},{193,1... | collective-permute-start | bytes 2555912 | tf_op jit(solution)/shard_map/ppermute | solution.py:76
  42.9 38.0 %collective-permute-start = (bf16[104,4096]{1,0:T(8,128)(2,1)S(1)}, bf16[104,4096]{1,0:T(8,128)(2,1)S(1)}, u32[]{:S(2)}, u32[]{:S(2)}) collective-permute-start(bf16[104,4096]{1,0:T(8,128)(2,1)S(1)} %constant_dynamic-update-slice_fusion), channel_id=1, source_target_pairs={{0,32},{32,0},{1,33},{33,1},{2,34},{34,2},{3,35},{35,3},{4,36},{36... | collective-permute-start | bytes 2555912 | tf_op jit(solution)/shard_map/ppermute | solution.py:76
  74.0 1.6 copy-start.7
  83.6 20.9 %collective-permute-start.1 = (bf16[104,4096]{1,0:T(8,128)(2,1)S(1)}, bf16[104,4096]{1,0:T(8,128)(2,1)S(1)}, u32[]{:S(2)}, u32[]{:S(2)}) collective-permute-start(bf16[104,4096]{1,0:T(8,128)(2,1)S(1)} %pad_maximum_fusion), channel_id=1, source_target_pairs={{0,32},{32,0},{1,33},{33,1},{2,34},{34,2},{3,35},{35,3},{4,36},{36... | collective-permute-start | bytes 2555912 | tf_op jit(solution)/shard_map/ppermute | solution.py:76
  84.2 3.1 %collective-permute-start.11 = (bf16[104,4096]{1,0:T(8,128)(2,1)S(1)}, bf16[104,4096]{1,0:T(8,128)(2,1)S(1)}, u32[]{:S(2)}, u32[]{:S(2)}) collective-permute-start(bf16[104,4096]{1,0:T(8,128)(2,1)S(1)} %collective-permute-done.10), channel_id=1, source_target_pairs={{0,32},{32,0},{1,33},{33,1},{2,34},{34,2},{3,35},{35,3},{4,36},{36... | collective-permute-start | bytes 2555912 | tf_op jit(solution)/shard_map/ppermute | solution.py:76
  84.8 5.4 %collective-permute-start.7 = (bf16[104,4096]{1,0:T(8,128)(2,1)S(1)}, bf16[104,4096]{1,0:T(8,128)(2,1)S(1)}, u32[]{:S(2)}, u32[]{:S(2)}) collective-permute-start(bf16[104,4096]{1,0:T(8,128)(2,1)S(1)} %collective-permute-done.6), channel_id=1, source_target_pairs={{0,32},{32,0},{1,33},{33,1},{2,34},{34,2},{3,35},{35,3},{4,36},{36... | collective-permute-start | bytes 2555912 | tf_op jit(solution)/shard_map/ppermute | solution.py:76
  85.1 5.9 %collective-permute-start.3 = (bf16[104,4096]{1,0:T(8,128)(2,1)S(1)}, bf16[104,4096]{1,0:T(8,128)(2,1)S(1)}, u32[]{:S(2)}, u32[]{:S(2)}) collective-permute-start(bf16[104,4096]{1,0:T(8,128)(2,1)S(1)} %collective-permute-done.2), channel_id=1, source_target_pairs={{0,32},{32,0},{1,33},{33,1},{2,34},{34,2},{3,35},{35,3},{4,36},{36... | collective-permute-start | bytes 2555912 | tf_op jit(solution)/shard_map/ppermute | solution.py:76
  90.0 10.4 %collective-permute-start.12 = (bf16[104,4096]{1,0:T(8,128)(2,1)S(1)}, bf16[104,4096]{1,0:T(8,128)(2,1)S(1)}, u32[]{:S(2)}, u32[]{:S(2)}) collective-permute-start(bf16[104,4096]{1,0:T(8,128)(2,1)S(1)} %pad_maximum_fusion.3), channel_id=1, source_target_pairs={{0,32},{32,0},{1,33},{33,1},{2,34},{34,2},{3,35},{35,3},{4,36},{36... | collective-permute-start | bytes 2555912 | tf_op jit(solution)/shard_map/ppermute | solution.py:76
  93.6 2.6 %collective-permute-start.4 = (bf16[104,4096]{1,0:T(8,128)(2,1)S(1)}, bf16[104,4096]{1,0:T(8,128)(2,1)S(1)}, u32[]{:S(2)}, u32[]{:S(2)}) collective-permute-start(bf16[104,4096]{1,0:T(8,128)(2,1)S(1)} %pad_maximum_fusion.1), channel_id=1, source_target_pairs={{0,32},{32,0},{1,33},{33,1},{2,34},{34,2},{3,35},{35,3},{4,36},{36... | collective-permute-start | bytes 2555912 | tf_op jit(solution)/shard_map/ppermute | solution.py:76
  96.0 3.5 %collective-permute-start.8 = (bf16[104,4096]{1,0:T(8,128)(2,1)S(1)}, bf16[104,4096]{1,0:T(8,128)(2,1)S(1)}, u32[]{:S(2)}, u32[]{:S(2)}) collective-permute-start(bf16[104,4096]{1,0:T(8,128)(2,1)S(1)} %pad_maximum_fusion.2), channel_id=1, source_target_pairs={{0,32},{32,0},{1,33},{33,1},{2,34},{34,2},{3,35},{35,3},{4,36},{36... | collective-permute-start | bytes 2555912 | tf_op jit(solution)/shard_map/ppermute | solution.py:76
  96.4 40.1 %collective-permute-start.5 = (bf16[104,4096]{1,0:T(8,128)(2,1)S(1)}, bf16[104,4096]{1,0:T(8,128)(2,1)S(1)}, u32[]{:S(2)}, u32[]{:S(2)}) collective-permute-start(bf16[104,4096]{1,0:T(8,128)(2,1)S(1)} %fusion.47), channel_id=1, source_target_pairs={{0,192},{64,0},{128,64},{192,128},{1,193},{65,1},{129,65},{193,129... | collective-permute-start | bytes 2555912 | tf_op jit(solution)/shard_map/ppermute | solution.py:76
  99.7 36.8 %collective-permute-start.9 = (bf16[104,4096]{1,0:T(8,128)(2,1)S(1)}, bf16[104,4096]{1,0:T(8,128)(2,1)S(1)}, u32[]{:S(2)}, u32[]{:S(2)}) collective-permute-start(bf16[104,4096]{1,0:T(8,128)(2,1)S(1)} %fusion.48), channel_id=1, source_target_pairs={{0,128},{64,192},{128,0},{192,64},{1,129},{65,193},{129,1},{193,65... | collective-permute-start | bytes 2555912 | tf_op jit(solution)/shard_map/ppermute | solution.py:76
  100.5 40.0 %collective-permute-start.13 = (bf16[104,4096]{1,0:T(8,128)(2,1)S(1)}, bf16[104,4096]{1,0:T(8,128)(2,1)S(1)}, u32[]{:S(2)}, u32[]{:S(2)}) collective-permute-start(bf16[104,4096]{1,0:T(8,128)(2,1)S(1)} %fusion.49), channel_id=1, source_target_pairs={{0,64},{64,128},{128,192},{192,0},{1,65},{65,129},{129,193},{193,1... | collective-permute-start | bytes 2555912 | tf_op jit(solution)/shard_map/ppermute | solution.py:76
  145.0 30.4 %all-to-all-start.1 = ((bf16[32,3,32,128]{3,2,1,0:T(8,128)(2,1)}), bf16[32,3,32,128]{3,2,1,0:T(8,128)(2,1)S(1)}, u32[]{:S(2)}, u32[]{:S(2)}) async-start(bf16[32,3,32,128]{3,2,1,0:T(8,128)(2,1)} %bitcast.12), calls=%async_computation.1 | async-start | bytes 1572864 | tf_op jit(solution)/shard_map/all_to_all | solution.py:109
  175.3 0.9 copy-start.5
